TPU v7x, 32 devices: a whole 2x2x4 slice. The times are simulated.
32 devices in a mesh: tok: 16 (over z, y, x), head: 2 (over core).
Axes of the slice: x: 2, y: 2, z: 4, core: 2. Of those that a mesh axis runs over, the one named last changes fastest.
Arguments:
- queries: bfloat16 [2, 4096, 512], P('head', 'tok'), may hold values from -6 to 6
- key_rows: bfloat16 [2, 4096, 512], P('head', 'tok'), may hold values from -6 to 6
- value_rows: bfloat16 [2, 4096, 512], P('head', 'tok'), may hold values from -6 to 6
- step_rates: float32 [2, 4096], P('head', 'tok'), may hold values from 0.1 to 1
- w_gate: bfloat16 [2, 512, 512], P('head'), may hold values from -0.25 to 0.25
- w_up: bfloat16 [2, 512, 512], P('head'), may hold values from -0.25 to 0.25
- w_down: bfloat16 [2, 512, 512], P('head'), may hold values from -0.25 to 0.25
- out_gain: float32 [2, 512], P('head'), may hold values from 0.1 to 1.9
- cotangent: bfloat16 [2, 4096, 512], P('head', 'tok'), may hold values from -6 to 6
Outputs:
- grad_queries: bfloat16 [2, 4096, 512], P('head', 'tok')
- grad_keys: bfloat16 [2, 4096, 512], P('head', 'tok')
- grad_values: bfloat16 [2, 4096, 512], P('head', 'tok')
- grad_gate: float32 [2, 512, 512], P('head', 'tok')
- grad_up: float32 [2, 512, 512], P('head', 'tok')
- grad_down: float32 [2, 512, 512], P('head', 'tok')
All inputs are finite; a program needn't handle non-finite values.
Results may differ from a plain program's by a relative error of at most 0.03.
Values sent between devices are 32-bit elements; how exact they have to be, the bound alone decides.
A program may use at most 128 MiB of HBM per device.

v0:
```python
import jax
import jax.numpy as jnp
from jax import lax
from jax.sharding import PartitionSpec as P

NS_STEPS = 3
coef_first = 3.4445
coef_second = -4.775
coef_third = 2.0315
inner_step = 0.5


def contract_rows(first_op, second_op):
    return lax.dot_general(
        first_op, second_op, (((0,), (0,)), ((), ())), preferred_element_type=jnp.float32
    )


def contract_cols(first_op, second_op):
    return lax.dot_general(
        first_op, second_op, (((1,), (1,)), ((), ())), preferred_element_type=jnp.float32
    )


def silu_parts(pre_gate):
    sigma_gate = jax.nn.sigmoid(pre_gate)
    act_gate = pre_gate * sigma_gate
    slope_gate = sigma_gate * (1.0 + pre_gate * (1.0 - sigma_gate))
    return (act_gate, slope_gate, sigma_gate)


def orthogonalize(matrix):
    current = matrix / jnp.sqrt(jnp.sum(matrix * matrix) + 1e-06)
    for iteration in range(NS_STEPS):
        narrow = current.astype(jnp.bfloat16)
        gram_matrix = contract_cols(narrow, narrow)
        gram_low = gram_matrix.astype(jnp.bfloat16)
        poly_term = (
            coef_second * gram_matrix
            + coef_third * jnp.dot(gram_low, gram_low, preferred_element_type=jnp.float32)
        ).astype(jnp.bfloat16)
        current = coef_first * current + jnp.dot(
            poly_term, narrow, preferred_element_type=jnp.float32
        )
    return current


def orthogonalize_all(grad_triple):
    mapped = jax.vmap(orthogonalize)
    return (mapped(grad_triple[0]), mapped(grad_triple[1]), mapped(grad_triple[2]))


def key_forward(w_gate, w_up, w_down, key_rows, value_rows, step_rates):
    key_gate = jnp.dot(key_rows, w_gate, preferred_element_type=jnp.float32)
    key_up = jnp.dot(key_rows, w_up, preferred_element_type=jnp.float32)
    act_gate, slope_gate, sigma_gate = silu_parts(key_gate)
    key_mixed = (act_gate * key_up).astype(jnp.bfloat16)
    target = (-step_rates[:, None] * value_rows).astype(jnp.bfloat16)
    key_mid = contract_cols(target, w_down)
    key_dgate = (key_mid * key_up * slope_gate).astype(jnp.bfloat16)
    key_dup = (key_mid * act_gate).astype(jnp.bfloat16)
    inner_grads = (
        contract_rows(key_rows, key_dgate),
        contract_rows(key_rows, key_dup),
        contract_rows(key_mixed, target),
    )
    stored = (
        key_gate,
        key_up,
        act_gate,
        slope_gate,
        sigma_gate,
        key_mixed,
        target,
        key_mid,
        key_dgate,
        key_dup,
    )
    return (inner_grads, stored)


def key_backward(w_gate, w_up, w_down, key_rows, step_rates, stored, back_a, back_b, back_c):
    (
        key_gate,
        key_up,
        act_gate,
        slope_gate,
        sigma_gate,
        key_mixed,
        target,
        key_mid,
        key_dgate,
        key_dup,
    ) = stored
    cot_a = back_a.astype(jnp.bfloat16)
    cot_b = back_b.astype(jnp.bfloat16)
    cot_c = back_c.astype(jnp.bfloat16)
    back_gate = jnp.dot(key_rows, cot_a, preferred_element_type=jnp.float32)
    back_up = jnp.dot(key_rows, cot_b, preferred_element_type=jnp.float32)
    back_mixed = contract_cols(target, cot_c)
    back_target = jnp.dot(key_mixed, cot_c, preferred_element_type=jnp.float32)
    curve_gate = sigma_gate * (1.0 - sigma_gate) * (2.0 + key_gate * (1.0 - 2.0 * sigma_gate))
    back_mid = (back_gate * key_up * slope_gate + back_up * act_gate).astype(jnp.bfloat16)
    gate_back = (
        back_gate * key_mid * key_up * curve_gate
        + back_up * key_mid * slope_gate
        + back_mixed * key_up * slope_gate
    ).astype(jnp.bfloat16)
    up_back = (back_gate * key_mid * slope_gate + back_mixed * act_gate).astype(jnp.bfloat16)
    key_grad = (
        contract_cols(key_dgate, cot_a)
        + contract_cols(key_dup, cot_b)
        + contract_cols(gate_back, w_gate)
        + contract_cols(up_back, w_up)
    )
    value_sum = back_target + jnp.dot(back_mid, w_down, preferred_element_type=jnp.float32)
    value_grad = (-step_rates[:, None] * value_sum).astype(jnp.bfloat16)
    weight_terms = jnp.concatenate(
        [
            contract_rows(key_rows, gate_back),
            contract_rows(key_rows, up_back),
            contract_rows(back_mid, target),
        ],
        axis=1,
    )
    return (key_grad.astype(jnp.bfloat16), value_grad, weight_terms)


def query_forward(new_gate, new_up, new_down, queries):
    query_gate = jnp.dot(queries, new_gate, preferred_element_type=jnp.float32)
    query_up = jnp.dot(queries, new_up, preferred_element_type=jnp.float32)
    act_gate, slope_gate, sigma_gate = silu_parts(query_gate)
    query_mixed = (act_gate * query_up).astype(jnp.bfloat16)
    output = jnp.dot(query_mixed, new_down, preferred_element_type=jnp.float32)
    return (output, (query_up, act_gate, slope_gate, query_mixed))


def query_backward(new_gate, new_up, new_down, queries, stored, grad_output):
    query_up, act_gate, slope_gate, query_mixed = stored
    query_mid = contract_cols(grad_output, new_down)
    query_dgate = (query_mid * query_up * slope_gate).astype(jnp.bfloat16)
    query_dup = (query_mid * act_gate).astype(jnp.bfloat16)
    query_grad = (contract_cols(query_dgate, new_gate) + contract_cols(query_dup, new_up)).astype(
        jnp.bfloat16
    )
    weight_terms = jnp.concatenate(
        [
            contract_rows(queries, query_dgate),
            contract_rows(queries, query_dup),
            contract_rows(query_mixed, grad_output),
        ],
        axis=1,
    )
    return (query_grad, weight_terms)


def local(queries, key_rows, value_rows, step_rates, w_gate, w_up, w_down, out_gain, cotangent):
    head_size = w_gate.shape[2]
    local_grads, stored = jax.vmap(key_forward)(
        w_gate, w_up, w_down, key_rows, value_rows, step_rates
    )
    inner_grads = lax.psum((local_grads[0], local_grads[1], local_grads[2]), "tok")
    unitary, ns_back = jax.vjp(orthogonalize_all, inner_grads)
    new_gate = (w_gate - inner_step * unitary[0]).astype(jnp.bfloat16)
    new_up = (w_up - inner_step * unitary[1]).astype(jnp.bfloat16)
    new_down = (w_down - inner_step * unitary[2]).astype(jnp.bfloat16)
    output, query_stored = jax.vmap(query_forward)(new_gate, new_up, new_down, queries)
    full_width = queries.shape[0] * lax.axis_size("head") * head_size
    squares_local = jnp.sum(output * output, axis=(0, 2))
    gain_wide = out_gain[:, None, :]
    squares, aligned = lax.psum(
        (squares_local, jnp.sum(cotangent * gain_wide * output, axis=(0, 2))), "head"
    )
    inverse_rms = lax.rsqrt(squares / full_width + 1e-05)
    grad_output = (
        gain_wide * cotangent * inverse_rms[None, :, None]
        - output * (aligned * inverse_rms * inverse_rms * inverse_rms / full_width)[None, :, None]
    ).astype(jnp.bfloat16)
    query_grad, query_terms = jax.vmap(query_backward)(
        new_gate, new_up, new_down, queries, query_stored, grad_output
    )
    share_rows = head_size // lax.axis_size("tok")
    query_whole = lax.psum(query_terms, "tok")
    query_share = lax.dynamic_slice_in_dim(
        query_whole, lax.axis_index("tok") * share_rows, share_rows, 1
    )
    outer_back = (
        -inner_step * query_whole[:, :, :head_size],
        -inner_step * query_whole[:, :, head_size : 2 * head_size],
        -inner_step * query_whole[:, :, 2 * head_size :],
    )
    back_triple = ns_back(outer_back)[0]
    key_grad, value_grad, key_terms = jax.vmap(key_backward)(
        w_gate,
        w_up,
        w_down,
        key_rows,
        step_rates,
        stored,
        back_triple[0],
        back_triple[1],
        back_triple[2],
    )
    key_share = lax.psum_scatter(key_terms, "tok", scatter_dimension=1, tiled=True)
    weight_share = query_share + key_share
    return (
        query_grad,
        key_grad,
        value_grad,
        weight_share[:, :, :head_size],
        weight_share[:, :, head_size : 2 * head_size],
        weight_share[:, :, 2 * head_size :],
    )


def solution(mesh):
    in_specs = (
        P("head", "tok", None),
        P("head", "tok", None),
        P("head", "tok", None),
        P("head", "tok"),
        P("head", None, None),
        P("head", None, None),
        P("head", None, None),
        P("head", None),
        P("head", "tok", None),
    )
    out_specs = (
        P("head", "tok", None),
        P("head", "tok", None),
        P("head", "tok", None),
        P("head", "tok", None),
        P("head", "tok", None),
        P("head", "tok", None),
    )
    return jax.shard_map(local, mesh=mesh, in_specs=in_specs, out_specs=out_specs, check_vma=False)
```

profile of v0, /device:TPU:0, one launch (start us, length us, event | category | flops | bytes accessed | tf_op | source)
XLA Modules:
  0.0 571.0 jit_solution(9727249518634274139)
XLA Ops:
  8.1 1.3 fusion.266
  9.5 1.6 fusion.272
  11.1 2.4 multiply_convert_fusion.2
  13.6 1.3 convolution_bitcast_fusion.8
  14.9 1.4 convolution_bitcast_fusion.7
  16.3 1.4 convolution_bitcast_fusion.6
  17.8 1.1 copy.62
  18.9 1.1 copy.67
  20.0 1.0 copy.72
  21.0 146.9 %all-reduce.11.cloned.1.call-done = (f32[1,512,512]{1,2,0:T(8,128)}, f32[1,512,512]{1,2,0:T(8,128)}, f32[1,512,512]{1,2,0:T(8,128)}) async-done(((f32[1,512,512]{1,2,0:T(8,128)}, f32[1,512,512]{1,2,0:T(8,128)}, f32[1,512,512]{1,2,0:T(8,128)}), (f32[1,512,512]{1,2,0:T(8,128)}, f32[1,512,512]{1,2,0:T(8,128)}, f32[1,512,512]{1,2,0:T(8,128)})) %all-reduce.11.cloned.1.call-update) | async-done | bytes 3145744 | tf_op jit(solution)/shard_map/psum | solution.py:162
  167.9 2.1 multiply_reduce_fusion.5
  170.7 2.2 fusion.263
  176.9 1.3 fusion.26
  178.2 0.9 multiply_reduce_fusion.4
  180.7 0.8 copy-done.97
  183.0 0.8 copy-done.64
  184.7 1.2 fusion.29
  186.0 0.9 multiply_reduce_fusion.3
  190.7 0.8 copy-done.60
  194.9 1.2 multiply_convert_fusion.3
  197.1 0.8 copy-done.28
  198.0 2.5 all-reduce.2
  200.5 1.3 fusion.304
  201.8 1.3 convolution_bitcast_fusion.3
  203.1 1.8 multiply_convert_fusion
  206.0 2.0 pad_maximum_fusion
  208.5 145.7 %all-reduce.7.cloned.1.call-done = f32[1,512,1536]{1,2,0:T(8,128)} async-done(((f32[1,512,1536]{1,2,0:T(8,128)}), f32[1,512,1536]{1,2,0:T(8,128)}) %all-reduce.7.cloned.1.call-update) | async-done | bytes 3145744 | tf_op jit(solution)/shard_map/psum | solution.py:183
  354.2 1.8 convolution_convert_fusion.52
  356.1 1.7 fusion.39
  370.9 1.2 fusion.72
  372.1 1.3 convolution_convert_fusion.22
  379.9 1.2 fusion.81
  381.1 1.3 convolution_convert_fusion.4
  383.9 2.2 multiply_reduce_fusion.2
  386.7 1.9 fusion.49
  388.6 2.0 fusion.103
  391.9 2.1 multiply_reduce_fusion.1
  394.7 3.0 fusion.172
  397.7 1.1 convolution_bitcast_fusion.19
  401.1 1.3 multiply_reduce_fusion
  407.2 5.7 copy.106
  414.8 1.3 fusion.455
  416.1 2.0 fusion.161
  419.2 1.0 fusion.160
  420.6 1.0 fusion.162
  421.6 137.6 %all-reduce.9.cloned.1.call-done = f32[1,512,1536]{2,0,1:T(1,128)} async-done(((f32[1,512,1536]{2,0,1:T(1,128)}), f32[1,512,1536]{2,0,1:T(1,128)}) %all-reduce.9.cloned.1.call-update) | async-done | bytes 3145744
  559.2 0.9 constant_dynamic-slice_fusion
  560.4 1.4 dynamic-slice_add_fusion
  (305 shorter events, 49.9 us)
Async XLA Ops:
  7.2 160.8 %all-reduce.11.cloned.1.call-start = ((), (), s32[]{:S(2)}) async-start(), calls=%async_computation.2 | async-start | bytes 6291456 | tf_op jit(solution)/shard_map/psum | solution.py:162
  9.5 5.4 copy-start.89
  11.1 5.2 copy-start.91
  11.1 5.2 copy-start.46
  13.6 2.7 copy-start.75
  13.6 2.7 copy-start.73
  13.6 2.7 copy-start.77
  14.9 2.9 copy-start.20
  16.3 2.6 copy-start.54
  16.3 3.7 copy-start.29
  17.8 336.4 %all-reduce.7.cloned.1.call-start = ((), (), s32[]{:S(2)}) async-start(), calls=%async_computation | async-start | bytes 6291456 | tf_op jit(solution)/shard_map/psum | solution.py:183
  170.7 2.6 copy-start.33
  174.2 2.2 copy-start.6
  174.6 2.2 copy-start.14
  175.9 2.3 copy-start.35
  182.0 2.2 copy-start.4
  182.5 2.2 copy-start.10
  183.7 2.2 copy-start.31
  189.8 2.2 copy-start.2
  190.2 2.3 copy-start.8
  192.5 2.4 copy-start.12
  193.0 3.1 copy-start.62
  193.6 2.5 copy-start.22
  194.3 2.3 copy-start.94
  194.9 2.2 copy-start.50
  200.5 4.4 copy-start.49
  208.0 351.1 %all-reduce.9.cloned.1.call-start = ((), (), s32[]{:S(2)}) async-start(), calls=%async_computation.1 | async-start | bytes 6291456
  354.2 3.6 copy-start.19
  354.2 4.1 copy-start.1
  354.2 4.1 copy-start.71
  370.9 2.5 copy-start.44
  379.9 2.5 copy-start.42
  379.9 2.5 copy-start.41
  386.7 4.0 copy-start.102
  394.7 4.2 copy-start.38
  394.7 4.2 copy-start.72
  397.7 2.6 copy-start.24
  401.1 2.3 copy-start.47
  403.5 2.2 copy-start.26
  412.9 3.2 copy-start.51
  412.9 5.3 copy-start.25
  412.9 5.3 copy-start.78
  412.9 5.6 copy-start.53
  412.9 5.6 copy-start.76
  412.9 5.9 %copy-start.21 = (bf16[1,512,512]{2,1,0:T(8,128)(2,1)S(1)}, bf16[1,512,512]{2,1,0:T(8,128)(2,1)}, u32[]{:S(2)}) copy-start(bf16[1,512,512]{2,1,0:T(8,128)(2,1)} %param.13) | copy-start | bytes 1572868
  414.8 4.0 copy-start.81
  416.1 3.1 copy-start.55
  416.1 3.1 copy-start.87
  (61 other events, 81.7 us)
Sparse Core Ops, SparseCore 0:
  17.9 149.9 all-reduce.10
  208.2 146.0 all-reduce.6
  413.0 146.1 all-reduce.8
where the time goes:
time: 582 us; the launch traced here: 571 us
  waiting for transfers between devices  430 us (74%)
  matrix products  79.5 us (14%)
  local copies, waits for them, and re-layouts  24.8 us (4%)
  between operations  20.8 us (4%)
  other arithmetic  12.9 us (2%)
    psum x1, waiting for transfers between devices, local(): lax.psum((local_grads[0], local_grads[1], local_grads[2]), 'tok')  147 us
    psum x1, waiting for transfers between devices, local(): query_whole = lax.psum(query_terms, 'tok')  146 us
    unnamed x4, waiting for transfers between devices  138 us
    dot_general x36, matrix products, contract_cols(): lax.dot_general(first_op, second_op, (((1,), (1,)), ((), ())), preferred_...  27.5 us
    unnamed x220, local copies, waits for them, and re-layouts  18.8 us
    dot_general x27, matrix products, orthogonalize(): jnp.dot(gram_low, gram_low, preferred_element_type=jnp.float32)  18.8 us
    dot_general x27, matrix products, orthogonalize(): jnp.dot(poly_term, narrow, preferred_element_type=jnp.float32)  17.2 us
  transfers between devices with their start and end apart: 3, of which 3 were waited for; matrix products, arithmetic and copies ran while one was open for 2% of the time, Pallas kernels for 0%

commit v1 on v0

--- a/solution.py
+++ b/solution.py
@@ -180,7 +180,13 @@
         new_gate, new_up, new_down, queries, query_stored, grad_output
     )
     share_rows = head_size // lax.axis_size("tok")
-    query_whole = lax.psum(query_terms, "tok")
+
+    def remake_regions(block_in):
+        reply = jax.lax.all_gather(block_in, "tok")
+        base_arr = jnp.sum(reply, axis=0)
+        return base_arr
+
+    query_whole = remake_regions(query_terms)
     query_share = lax.dynamic_slice_in_dim(
         query_whole, lax.axis_index("tok") * share_rows, share_rows, 1
     )

time: 582 us -> 973 us (1.67)
  waiting for transfers between devices: 430 us -> 791 us
  other arithmetic: 12.9 us -> 30.2 us
  blocking collectives: 2.47 us -> 13.2 us
    all_gather x0 -> x1, waiting for transfers between devices: none -> 508 us  [remake_regions(): reply = jax.lax.all_gather(block_in, 'tok')]
    psum x1 -> x0, waiting for transfers between devices: 146 us -> none  [local(): query_whole = lax.psum(query_terms, 'tok')]
    reduce_sum x0 -> x1, other arithmetic: none -> 20.5 us  [remake_regions(): base_arr = jnp.sum(reply, axis=0)]
    psum x1, blocking collectives: 2.47 us -> 13.2 us  [local(): lax.psum((squares_local, jnp.sum(cotangent * gain_wide * output, axis=(0,...]
  transfers between devices with their start and end apart: 3 -> 3, of which waited for: 3 -> 3; matrix products, arithmetic and copies ran while one was open for 2% -> 1% of each run, Pallas kernels for 0% -> 0%
where the time goes in v1:
time: 973 us; the launch traced here: 963 us
  waiting for transfers between devices  791 us (81%)
  matrix products  77.1 us (8%)
  local copies, waits for them, and re-layouts  30.2 us (3%)
  other arithmetic  30.2 us (3%)
  between operations  20.9 us (2%)
  blocking collectives  13.2 us (1%)
    all_gather x1, waiting for transfers between devices, remake_regions(): reply = jax.lax.all_gather(block_in, 'tok')  508 us
    psum x1, waiting for transfers between devices, local(): lax.psum((local_grads[0], local_grads[1], local_grads[2]), 'tok')  147 us
    unnamed x4, waiting for transfers between devices  137 us
    dot_general x36, matrix products, contract_cols(): lax.dot_general(first_op, second_op, (((1,), (1,)), ((), ())), preferred_...  27.1 us
    reduce_sum x1, other arithmetic, remake_regions(): base_arr = jnp.sum(reply, axis=0)  20.5 us
  transfers between devices with their start and end apart: 3, of which 3 were waited for; matrix products, arithmetic and copies ran while one was open for 1% of the time, Pallas kernels for 0%

profile of v1, /device:TPU:0, one launch (start us, length us, event | category | flops | bytes accessed | tf_op | source)
XLA Modules:
  0.0 962.8 jit_solution(17140118895210348814)
XLA Ops:
  8.1 1.3 fusion.266
  9.5 1.6 fusion.272
  11.2 2.4 multiply_convert_fusion.2
  13.6 1.3 convolution_bitcast_fusion.8
  14.9 1.3 convolution_bitcast_fusion.7
  16.2 1.4 convolution_bitcast_fusion.6
  17.7 1.0 copy.159
  18.7 1.1 copy.164
  19.8 1.0 copy.169
  20.8 146.9 %all-reduce.8.cloned.1.call-done = (f32[1,512,512]{1,2,0:T(8,128)}, f32[1,512,512]{1,2,0:T(8,128)}, f32[1,512,512]{1,2,0:T(8,128)}) async-done(((f32[1,512,512]{1,2,0:T(8,128)}, f32[1,512,512]{1,2,0:T(8,128)}, f32[1,512,512]{1,2,0:T(8,128)}), (f32[1,512,512]{1,2,0:T(8,128)}, f32[1,512,512]{1,2,0:T(8,128)}, f32[1,512,512]{1,2,0:T(8,128)})) %all-reduce.8.cloned.1.call-update) | async-done | bytes 3145744 | tf_op jit(solution)/shard_map/psum | solution.py:162
  167.7 2.1 multiply_reduce_fusion.5
  170.5 2.1 fusion.263
  172.7 1.1 copy-done.47
  177.7 1.3 fusion.26
  179.0 0.9 multiply_reduce_fusion.4
  181.0 1.0 copy-done.45
  182.5 0.8 copy-done.99
  186.5 1.2 fusion.29
  187.7 0.9 multiply_reduce_fusion.3
  192.0 1.0 copy-done.13
  197.7 1.2 multiply_convert_fusion.3
  199.9 13.2 %all-reduce.2 = (f32[256]{0:T(256)S(1)}, f32[256]{0:T(256)S(1)}) all-reduce(f32[256]{0:T(256)S(1)} %get-tuple-element.39, f32[256]{0:T(256)S(1)} %multiply_reduce_fusion.6), channel_id=1, replica_groups=mesh['tok'=16,'head'=2] {'head'}, use_global_device_ids=true, to_apply=%region_9.0 | all-reduce | flops 512 | bytes 4096 | tf_op jit(solution)/shard_map/psum | solution.py:171
  213.6 1.5 multiply_convert_fusion
  216.5 2.4 copy.174
  219.2 507.7 %all-gather.3.cloned.1.call-done = f32[16,512,1536]{2,1,0:T(8,128)} async-done(((f32[1,512,1536]{2,1,0:T(8,128)}), f32[16,512,1536]{2,1,0:T(8,128)}) %all-gather.3.cloned.1.call-update) | async-done | bytes 50331664 | tf_op jit(solution)/shard_map/all_gather | solution.py:185
  726.9 20.5 %reduce.9 = f32[512,1536]{1,0:T(8,128)} reduce(f32[16,512,1536]{2,1,0:T(8,128)} %all-gather.3.cloned.1.call-done, f32[]{:T(128)} %constant.38.clone.1), dimensions={0}, to_apply=%region_10.0 | reduce | flops 11796480 | bytes 53477380 | tf_op jit(solution)/shard_map/reduce_sum | solution.py:186
  747.5 2.4 copy.175
  749.9 1.6 fusion.57
  751.4 1.8 convolution_convert_fusion.52
  766.5 1.2 fusion.72
  767.7 1.3 convolution_convert_fusion.22
  775.7 1.2 fusion.81
  777.0 1.3 convolution_convert_fusion.4
  779.7 2.1 multiply_reduce_fusion.2
  782.5 1.6 fusion.49
  784.1 1.7 fusion.103
  787.1 2.1 multiply_reduce_fusion.1
  789.9 3.0 fusion.172
  792.9 1.1 convolution_bitcast_fusion.19
  796.3 1.3 multiply_reduce_fusion
  802.3 5.6 copy.205
  809.9 1.3 fusion.455
  811.2 2.1 fusion.161
  814.4 1.0 fusion.160
  815.8 1.0 fusion.162
  816.8 136.5 %all-reduce.6.cloned.1.call-done = f32[1,512,1536]{2,0,1:T(1,128)} async-done(((f32[1,512,1536]{2,0,1:T(1,128)}), f32[1,512,1536]{2,0,1:T(1,128)}) %all-reduce.6.cloned.1.call-update) | async-done | bytes 3145744
  953.3 0.9 constant_dynamic-slice_fusion
  954.3 1.0 bitcast_add_fusion
  (308 shorter events, 50.6 us)
Async XLA Ops:
  7.2 160.6 %all-reduce.8.cloned.1.call-start = ((), (), s32[]{:S(2)}) async-start(), calls=%async_computation.2 | async-start | bytes 6291456 | tf_op jit(solution)/shard_map/psum | solution.py:162
  9.5 5.4 copy-start.92
  11.1 5.1 copy-start.94
  11.1 5.1 copy-start.53
  13.6 2.6 copy-start.79
  13.6 2.6 copy-start.77
  13.6 2.6 copy-start.81
  14.9 2.8 copy-start.25
  16.2 2.5 copy-start.60
  16.2 3.6 copy-start.33
  17.6 709.3 %all-gather.3.cloned.1.call-start = ((), (), s32[]{:S(2)}) async-start(), calls=%async_computation | async-start | bytes 53477376 | tf_op jit(solution)/shard_map/all_gather | solution.py:185
  170.5 3.6 copy-start.37
  175.4 2.2 copy-start.21
  176.7 2.3 copy-start.40
  177.2 18.5 %copy-start.5 = (f32[1,512,512]{1,2,0:T(8,128)}, f32[1,512,512]{1,2,0:T(8,128)S(1)}, u32[]{:S(2)}) copy-start(f32[1,512,512]{1,2,0:T(8,128)S(1)} %fusion.10) | copy-start | bytes 3145732
  183.8 2.2 copy-start.9
  184.2 2.2 copy-start.15
  185.5 2.2 copy-start.35
  186.0 10.7 %copy-start.3 = (f32[1,512,512]{1,2,0:T(8,128)}, f32[1,512,512]{1,2,0:T(8,128)S(1)}, u32[]{:S(2)}) copy-start(f32[1,512,512]{1,2,0:T(8,128)S(1)} %fusion.15) | copy-start | bytes 3145732
  191.5 3.2 copy-start.7
  194.7 4.1 copy-start.1
  195.2 2.4 copy-start.17
  195.7 3.1 copy-start.69
  196.3 2.5 copy-start.27
  218.9 734.4 %all-reduce.6.cloned.1.call-start = ((), (), s32[]{:S(2)}) async-start(), calls=%async_computation.1 | async-start | bytes 6291456
  749.9 3.4 copy-start.24
  751.4 2.8 copy-start.6
  766.5 2.5 copy-start.51
  766.5 2.5 copy-start.70
  775.7 2.5 copy-start.49
  775.7 2.5 copy-start.48
  779.7 2.9 copy-start.46
  781.8 4.1 copy-start.42
  782.5 3.3 copy-start.104
  787.1 2.8 copy-start.39
  789.9 4.2 copy-start.44
  789.9 4.2 copy-start.76
  792.9 2.6 copy-start.29
  796.3 2.3 copy-start.54
  808.0 3.2 copy-start.57
  808.0 5.3 copy-start.30
  808.0 5.3 copy-start.82
  808.0 5.6 copy-start.59
  808.0 5.6 copy-start.80
  808.1 5.9 copy-start.26
  809.9 4.1 copy-start.85
  811.2 3.2 copy-start.61
  811.2 3.2 copy-start.91
  (63 other events, 84.0 us)
Sparse Core Ops, SparseCore 0:
  17.8 149.9 all-reduce.7
  219.1 507.8 all-gather.2
  808.2 145.1 all-reduce.5
